TPU v7x, 512 devices: a whole 4x8x8 slice. The times are simulated.
512 devices in a mesh: gx: 16 (over y_hi, z), gy: 4 (over y_lo), gz: 8 (over x, core).
Axes of the slice: x: 4, y: 8 (y_hi: 2, y_lo: 4; y = y_hi * 4 + y_lo), z: 8, core: 2. Of those that a mesh axis runs over, the one named last changes fastest.
Arguments:
- field: float32 [4, 128, 512, 512], P(None, ('gx', 'gz'), 'gy'), may hold values from -6 to 6
- brick_order: int32 [32], replicated, may hold values from 0 to 31, each once
- start_first: float32 [128, 32], replicated, may hold values from -6 to 6
- start_second: float32 [512, 32], replicated, may hold values from -6 to 6
- start_third: float32 [512, 32], replicated, may hold values from -6 to 6
Outputs:
- core: float32 [128, 32, 32], P(('gx', 'gy'), 'gz')
Inputs may be any that keep to these rules, and one draw needn't show every extreme that they name: `brick_order`: each of 0 to 31 appears exactly once.
All inputs are finite; a program needn't handle non-finite values.
Results may differ from a plain program's by a relative error of at most 0.0003.
Values sent between devices are 32-bit elements; how exact they have to be, the bound alone decides.
No kernel may reach another device: no remote copies, remote signals or barrier semaphores. Data moves between devices by JAX's collectives and lax.ppermute only.
A program may use at most 64 MiB of HBM per device.

v0:
```python
import jax
import jax.numpy as jnp
from jax import lax
from jax.sharding import PartitionSpec as P

ITERS = 2
highest = lax.Precision.HIGHEST


def orthonormal(columns):
    inner_gram = jnp.dot(columns.T, columns, precision=highest)
    factor_low = jnp.linalg.cholesky(inner_gram)
    return jax.scipy.linalg.solve_triangular(factor_low, columns.T, lower=True).T


def subspace(gram_mat, initial):
    current = initial
    for repeat in range(ITERS):
        current = orthonormal(jnp.dot(gram_mat, current, precision=highest))
    return current


def shards(field, brick_order, start_first, start_second, start_third):
    species, rows_x, cells_y, cells_z = field.shape
    count_gx = lax.axis_size("gx")
    count_gy = lax.axis_size("gy")
    count_gz = lax.axis_size("gz")
    brick_count = brick_order.shape[0]
    brick_len = cells_z // count_gz
    small_len = cells_z // brick_count
    cut_y = cells_y // count_gx
    onehot = (brick_order[:, None] == lax.iota(jnp.int32, brick_count)[None, :]).astype(jnp.float32)
    stored = field.reshape(species, rows_x, cells_y, brick_count, small_len)
    placed = jnp.einsum("sxybc,bg->sxygc", stored, onehot, precision=highest).reshape(
        species, rows_x, cells_y, cells_z
    )
    taper = 0.5 + 1.5 * lax.iota(jnp.float32, cells_z) / (cells_z - 1)
    placed = placed * taper
    grid_block = lax.all_to_all(placed, "gz", split_axis=3, concat_axis=1, tiled=True)
    spread = lax.all_to_all(grid_block, "gx", split_axis=2, concat_axis=1, tiled=True)
    local_first = jnp.einsum("sxyz,swyz->xw", spread, spread, precision=highest)
    gram_first = lax.psum(local_first, ("gx", "gy", "gz"))
    factor_first = subspace(gram_first, start_first)
    rank_one = factor_first.shape[1]
    after_first = jnp.einsum("sxyz,xr->sryz", spread, factor_first, precision=highest)
    after_first = after_first.reshape(species * rank_one, cut_y, brick_len)
    regrouped = lax.all_to_all(after_first, ("gx", "gy"), split_axis=0, concat_axis=1, tiled=True)
    merged_rows = regrouped.shape[0]
    regrouped = regrouped.reshape(merged_rows, count_gx, count_gy, cut_y, brick_len)
    second_fibres = jnp.transpose(regrouped, (0, 2, 1, 3, 4)).reshape(
        merged_rows, count_gy * count_gx * cut_y, brick_len
    )
    local_second = jnp.einsum("myz,muz->yu", second_fibres, second_fibres, precision=highest)
    gram_second = lax.psum(local_second, ("gx", "gy", "gz"))
    factor_second = subspace(gram_second, start_second)
    after_second = jnp.einsum("myz,yq->mqz", second_fibres, factor_second, precision=highest)
    third_fibres = lax.all_to_all(after_second, "gz", split_axis=1, concat_axis=2, tiled=True)
    local_third = jnp.einsum("mqz,mqw->zw", third_fibres, third_fibres, precision=highest)
    gram_third = lax.psum(local_third, ("gx", "gy", "gz"))
    factor_third = subspace(gram_third, start_third)
    return jnp.einsum("mqz,zt->mqt", third_fibres, factor_third, precision=highest)


def solution(mesh):
    in_specs = (P(None, ("gx", "gz"), "gy", None), P(), P(), P(), P())
    out_specs = P(("gx", "gy"), "gz", None)
    return jax.shard_map(shards, mesh=mesh, in_specs=in_specs, out_specs=out_specs, check_vma=False)
```

profile of v0, /device:TPU:24, one launch (start us, length us, event | category | flops | bytes accessed | tf_op | source)
XLA Modules:
  0.0 976.2 jit_solution(7257902330931354419)
XLA Ops:
  6.6 1.6 copy.35
  10.6 20.2 %all_to_all.69 = f32[4,1,128,512]{2,0,1,3:T(4,128)S(1)} all-to-all(f32[4,1,128,512]{2,0,1,3:T(4,128)S(1)} %copy.38), channel_id=1, replica_groups=mesh['gx'=16,'gy'=4,'gz'=8] {'gz'}, dimensions={3} | all-to-all | bytes 2097152 | tf_op jit(solution)/shard_map/all_to_all | solution.py:39
  30.9 1.8 copy.40
  32.7 1.3 reshape.62
  34.0 39.6 %all_to_all.70 = f32[16,1,16384]{2,1,0:T(1,128)S(1)} all-to-all(f32[16,1,16384]{2,1,0:T(1,128)S(1)} %reshape.62), channel_id=1, replica_groups=mesh['gx'=16,'gy'=4,'gz'=8] {'gx'}, dimensions={0} | all-to-all | bytes 2097152 | tf_op jit(solution)/shard_map/all_to_all | solution.py:40
  74.1 3.1 reduce.4
  78.1 2.6 copy.42
  80.7 2.2 copy.43
  82.9 2.4 convolution_bitcast_fusion.6
  85.4 256.2 %all-reduce.4.cloned.1.call-done = f32[128,128]{1,0:T(8,128)} async-done(((f32[128,128]{1,0:T(8,128)}), f32[128,128]{1,0:T(8,128)}) %all-reduce.4.cloned.1.call-update) | async-done | bytes 65552 | tf_op jit(solution)/shard_map/psum | solution.py:42
  342.9 2.9 cholesky.104
  347.2 2.4 custom-call.12
  351.2 2.9 cholesky.115
  355.5 2.4 custom-call.13
  358.2 2.9 convolution_bitcast_fusion.3
  361.8 20.5 %all_to_all.71 = f32[64,1,1024]{2,1,0:T(1,128)S(1)} all-to-all(f32[64,1,1024]{2,1,0:T(1,128)S(1)} %reshape.64), channel_id=1, replica_groups=mesh['gx'=16,'gy'=4,'gz'=8] {'gx','gy'}, dimensions={0} | all-to-all | bytes 524288 | tf_op jit(solution)/shard_map/all_to_all | solution.py:47
  382.3 1.3 reduce.5
  383.7 2.1 convolution_bitcast_fusion.1
  385.9 266.8 %all-reduce.6.cloned.1.call-done = f32[512,512]{1,0:T(8,128)} async-done(((f32[512,512]{1,0:T(8,128)}), f32[512,512]{1,0:T(8,128)}) %all-reduce.6.cloned.1.call-update) | async-done | bytes 1048592 | tf_op jit(solution)/shard_map/psum | solution.py:54
  652.7 2.4 fusion.41
  655.3 2.9 cholesky.126
  659.7 2.4 custom-call.14
  663.8 2.9 cholesky.137
  668.2 2.4 custom-call.15
  671.4 9.2 all_to_all.72
  681.5 2.1 convolution_bitcast_fusion
  683.6 267.3 %all-reduce.8.cloned.1.call-done = f32[512,512]{1,0:T(8,128)} async-done(((f32[512,512]{1,0:T(8,128)}), f32[512,512]{1,0:T(8,128)}) %all-reduce.8.cloned.1.call-update) | async-done | bytes 1048592 | tf_op jit(solution)/shard_map/psum | solution.py:59
  950.8 2.4 fusion.45
  953.5 2.9 cholesky.148
  957.8 2.4 custom-call.16
  961.9 2.9 cholesky.159
  966.1 2.4 custom-call.17
  (84 shorter events, 22.6 us)
Async XLA Ops:
  6.5 646.1 %copy-start = (f32[512,32]{0,1:T(8,128)S(1)}, f32[512,32]{0,1:T(8,128)}, u32[]{:S(2)}) copy-start(f32[512,32]{0,1:T(8,128)} %param.13) | copy-start | bytes 196612
  6.5 1.6 copy-start.5
  6.5 335.1 %all-reduce.4.cloned.1.call-start = ((), (), s32[]{:S(2)}) async-start(), calls=%async_computation.4 | async-start | bytes 131072 | tf_op jit(solution)/shard_map/psum | solution.py:42
  80.7 260.9 %copy-start.4 = (f32[128,32]{0,1:T(8,128)S(1)}, f32[128,32]{0,1:T(8,128)}, u32[]{:S(2)}) copy-start(f32[128,32]{0,1:T(8,128)} %param.12) | copy-start | bytes 49156
  85.4 567.3 %all-reduce.6.cloned.1.call-start = ((), (), s32[]{:S(2)}) async-start(), calls=%async_computation.5 | async-start | bytes 2097152 | tf_op jit(solution)/shard_map/psum | solution.py:54
  385.8 565.0 %all-reduce.8.cloned.1.call-start = ((), (), s32[]{:S(2)}) async-start(), calls=%async_computation.6 | async-start | bytes 2097152 | tf_op jit(solution)/shard_map/psum | solution.py:59
  652.7 9.8 %copy-start.1 = (f32[512,512]{1,0:T(8,128)S(1)}, f32[512,512]{1,0:T(8,128)}, u32[]{:S(2)}) copy-start(f32[512,512]{1,0:T(8,128)} %all-reduce.6.cloned.1.call-done) | copy-start | bytes 3145732
  662.4 288.4 %copy-start.3 = (f32[512,32]{0,1:T(8,128)S(1)}, f32[512,32]{0,1:T(8,128)}, u32[]{:S(2)}) copy-start(f32[512,32]{0,1:T(8,128)} %param.14) | copy-start | bytes 196612
  950.8 9.6 copy-start.2
Sparse Core Ops, SparseCore 0:
  85.5 256.0 all-reduce.3
  386.0 266.6 all-reduce.5
  683.7 267.0 all-reduce.7
where the time goes:
time: 977 us; the launch traced here: 976 us
  waiting for transfers between devices  790 us (81%)
  blocking collectives  89.5 us (9%)
  other arithmetic  45.7 us (5%)
  matrix products  23.3 us (2%)
  local copies, waits for them, and re-layouts  13.7 us (1%)
  between operations  13.5 us (1%)
    psum x1, waiting for transfers between devices, shards(): gram_third = lax.psum(local_third, ('gx', 'gy', 'gz'))  267 us
    psum x1, waiting for transfers between devices, shards(): gram_second = lax.psum(local_second, ('gx', 'gy', 'gz'))  267 us
    psum x1, waiting for transfers between devices, shards(): gram_first = lax.psum(local_first, ('gx', 'gy', 'gz'))  256 us
    all_to_all x1, blocking collectives, shards(): lax.all_to_all(grid_block, 'gx', split_axis=2, concat_axis=1, tiled=True)  39.6 us
    another operation x18, other arithmetic, orthonormal(): factor_low = jnp.linalg.cholesky(inner_gram)  21.9 us
    all_to_all x1, blocking collectives, shards(): lax.all_to_all(after_first, ('gx', 'gy'), split_axis=0, concat_axis=1, ti...  20.5 us
    all_to_all x1, blocking collectives, shards(): lax.all_to_all(placed, 'gz', split_axis=3, concat_axis=1, tiled=True)  20.2 us
  transfers between devices with their start and end apart: 3, of which 3 were waited for; matrix products, arithmetic and copies ran while one was open for 0% of the time, Pallas kernels for 0%

commit v1 on v0

--- a/solution.py
+++ b/solution.py
@@ -5,6 +5,13 @@
 
 ITERS = 2
 highest = lax.Precision.HIGHEST
+
+
+def stacked_exchange(shard, axis, split, join):
+    size = lax.axis_size(axis)
+    pieces = jnp.stack(jnp.split(shard, size, axis=split), axis=0)
+    pieces = lax.all_to_all(pieces, axis, split_axis=0, concat_axis=0)
+    return jnp.concatenate(pieces, axis=join)
 
 
 def orthonormal(columns):
@@ -44,7 +51,7 @@
     rank_one = factor_first.shape[1]
     after_first = jnp.einsum("sxyz,xr->sryz", spread, factor_first, precision=highest)
     after_first = after_first.reshape(species * rank_one, cut_y, brick_len)
-    regrouped = lax.all_to_all(after_first, ("gx", "gy"), split_axis=0, concat_axis=1, tiled=True)
+    regrouped = stacked_exchange(after_first, ("gx", "gy"), 0, 1)
     merged_rows = regrouped.shape[0]
     regrouped = regrouped.reshape(merged_rows, count_gx, count_gy, cut_y, brick_len)
     second_fibres = jnp.transpose(regrouped, (0, 2, 1, 3, 4)).reshape(

time: 977 us -> 978 us (level)
  no operation moved by 1% of the time
where the time goes in v1:
time: 978 us; the launch traced here: 977 us
  waiting for transfers between devices  790 us (81%)
  blocking collectives  89.7 us (9%)
  other arithmetic  45.7 us (5%)
  matrix products  23.3 us (2%)
  between operations  14 us (1%)
  local copies, waits for them, and re-layouts  13.9 us (1%)
    psum x1, waiting for transfers between devices, shards(): gram_third = lax.psum(local_third, ('gx', 'gy', 'gz'))  267 us
    psum x1, waiting for transfers between devices, shards(): gram_second = lax.psum(local_second, ('gx', 'gy', 'gz'))  267 us
    psum x1, waiting for transfers between devices, shards(): gram_first = lax.psum(local_first, ('gx', 'gy', 'gz'))  256 us
    all_to_all x1, blocking collectives, shards(): lax.all_to_all(grid_block, 'gx', split_axis=2, concat_axis=1, tiled=True)  39.6 us
    another operation x18, other arithmetic, orthonormal(): factor_low = jnp.linalg.cholesky(inner_gram)  21.9 us
    all_to_all x1, blocking collectives, stacked_exchange(): pieces = lax.all_to_all(pieces, axis, split_axis=0, concat_axis=0)  20.7 us
    all_to_all x1, blocking collectives, shards(): lax.all_to_all(placed, 'gz', split_axis=3, concat_axis=1, tiled=True)  20.2 us
  transfers between devices with their start and end apart: 3, of which 3 were waited for; matrix products, arithmetic and copies ran while one was open for 0% of the time, Pallas kernels for 0%

profile of v1, /device:TPU:24, one launch (start us, length us, event | category | flops | bytes accessed | tf_op | source)
XLA Modules:
  0.0 977.2 jit_solution(6537090241458984467)
XLA Ops:
  6.6 1.6 copy.35
  10.6 20.2 %all_to_all.59 = f32[4,1,128,512]{2,0,1,3:T(4,128)S(1)} all-to-all(f32[4,1,128,512]{2,0,1,3:T(4,128)S(1)} %copy.38), channel_id=1, replica_groups=mesh['gx'=16,'gy'=4,'gz'=8] {'gz'}, dimensions={3} | all-to-all | bytes 2097152 | tf_op jit(solution)/shard_map/all_to_all | solution.py:46
  30.9 1.8 copy.40
  32.7 1.3 reshape.61
  34.0 39.6 %all_to_all.60 = f32[16,1,16384]{2,1,0:T(1,128)S(1)} all-to-all(f32[16,1,16384]{2,1,0:T(1,128)S(1)} %reshape.61), channel_id=1, replica_groups=mesh['gx'=16,'gy'=4,'gz'=8] {'gx'}, dimensions={0} | all-to-all | bytes 2097152 | tf_op jit(solution)/shard_map/all_to_all | solution.py:47
  74.1 3.1 reduce.4
  78.1 2.6 copy.42
  80.7 2.2 copy.43
  82.9 2.4 convolution_bitcast_fusion.6
  85.4 256.2 %all-reduce.4.cloned.1.call-done = f32[128,128]{1,0:T(8,128)} async-done(((f32[128,128]{1,0:T(8,128)}), f32[128,128]{1,0:T(8,128)}) %all-reduce.4.cloned.1.call-update) | async-done | bytes 65552 | tf_op jit(solution)/shard_map/psum | solution.py:49
  342.9 2.9 cholesky.104
  347.2 2.4 custom-call.12
  351.2 2.9 cholesky.115
  355.5 2.4 custom-call.13
  358.2 2.9 convolution_bitcast_fusion.3
  362.5 20.7 %all_to_all.61 = f32[64,1,1024]{2,1,0:T(1,128)S(1)} all-to-all(f32[64,1,1024]{2,1,0:T(1,128)S(1)} %reshape.63), channel_id=1, replica_groups=mesh['gx'=16,'gy'=4,'gz'=8] {'gx','gy'}, dimensions={0} | all-to-all | bytes 524288 | tf_op jit(solution)/shard_map/all_to_all | solution.py:13
  383.2 1.3 reduce.5
  384.7 2.1 convolution_bitcast_fusion.1
  386.8 266.8 %all-reduce.6.cloned.1.call-done = f32[512,512]{1,0:T(8,128)} async-done(((f32[512,512]{1,0:T(8,128)}), f32[512,512]{1,0:T(8,128)}) %all-reduce.6.cloned.1.call-update) | async-done | bytes 1048592 | tf_op jit(solution)/shard_map/psum | solution.py:61
  653.7 2.4 fusion.41
  656.3 2.9 cholesky.126
  660.7 2.4 custom-call.14
  664.8 2.9 cholesky.137
  669.2 2.4 custom-call.15
  672.4 9.2 all_to_all.62
  682.5 2.1 convolution_bitcast_fusion
  684.6 267.3 %all-reduce.8.cloned.1.call-done = f32[512,512]{1,0:T(8,128)} async-done(((f32[512,512]{1,0:T(8,128)}), f32[512,512]{1,0:T(8,128)}) %all-reduce.8.cloned.1.call-update) | async-done | bytes 1048592 | tf_op jit(solution)/shard_map/psum | solution.py:66
  951.9 2.4 fusion.45
  954.5 2.9 cholesky.148
  958.8 2.4 custom-call.16
  962.9 2.9 cholesky.159
  967.2 2.4 custom-call.17
  (148 shorter events, 22.8 us)
Async XLA Ops:
  6.5 647.1 %copy-start = (f32[512,32]{0,1:T(8,128)S(1)}, f32[512,32]{0,1:T(8,128)}, u32[]{:S(2)}) copy-start(f32[512,32]{0,1:T(8,128)} %param.13) | copy-start | bytes 196612
  6.5 1.6 copy-start.5
  6.5 335.1 %all-reduce.4.cloned.1.call-start = ((), (), s32[]{:S(2)}) async-start(), calls=%async_computation.4 | async-start | bytes 131072 | tf_op jit(solution)/shard_map/psum | solution.py:49
  80.7 260.9 %copy-start.4 = (f32[128,32]{0,1:T(8,128)S(1)}, f32[128,32]{0,1:T(8,128)}, u32[]{:S(2)}) copy-start(f32[128,32]{0,1:T(8,128)} %param.12) | copy-start | bytes 49156
  85.4 568.3 %all-reduce.6.cloned.1.call-start = ((), (), s32[]{:S(2)}) async-start(), calls=%async_computation.5 | async-start | bytes 2097152 | tf_op jit(solution)/shard_map/psum | solution.py:61
  386.8 565.1 %all-reduce.8.cloned.1.call-start = ((), (), s32[]{:S(2)}) async-start(), calls=%async_computation.6 | async-start | bytes 2097152 | tf_op jit(solution)/shard_map/psum | solution.py:66
  653.7 9.8 copy-start.1
  663.4 288.5 %copy-start.3 = (f32[512,32]{0,1:T(8,128)S(1)}, f32[512,32]{0,1:T(8,128)}, u32[]{:S(2)}) copy-start(f32[512,32]{0,1:T(8,128)} %param.14) | copy-start | bytes 196612
  951.9 9.6 copy-start.2
Sparse Core Ops, SparseCore 0:
  85.5 256.0 all-reduce.3
  386.9 266.7 all-reduce.5
  684.7 267.1 all-reduce.7

commit v2 on v0

--- a/solution.py
+++ b/solution.py
@@ -5,6 +5,11 @@
 
 ITERS = 2
 highest = lax.Precision.HIGHEST
+
+
+def gather_and_add(x, axis):
+    parts = lax.all_gather(x, axis)
+    return jnp.sum(parts, axis=0)
 
 
 def orthonormal(columns):
@@ -39,7 +44,7 @@
     grid_block = lax.all_to_all(placed, "gz", split_axis=3, concat_axis=1, tiled=True)
     spread = lax.all_to_all(grid_block, "gx", split_axis=2, concat_axis=1, tiled=True)
     local_first = jnp.einsum("sxyz,swyz->xw", spread, spread, precision=highest)
-    gram_first = lax.psum(local_first, ("gx", "gy", "gz"))
+    gram_first = gather_and_add(local_first, ("gx", "gy", "gz"))
     factor_first = subspace(gram_first, start_first)
     rank_one = factor_first.shape[1]
     after_first = jnp.einsum("sxyz,xr->sryz", spread, factor_first, precision=highest)

time: 977 us -> 1590 us (1.63)
  waiting for transfers between devices: 790 us -> 1390 us
    all_gather x0 -> x1, waiting for transfers between devices: none -> 852 us  [gather_and_add(): parts = lax.all_gather(x, axis)]
    psum x1 -> x0, waiting for transfers between devices: 256 us -> none  [shards(): gram_first = lax.psum(local_first, ('gx', 'gy', 'gz'))]
where the time goes in v2:
time: 1590 us
  waiting for transfers between devices  1390 us (87%)
  blocking collectives  89.7 us (6%)
  other arithmetic  59 us (4%)
  matrix products  21.6 us (1%)
    all_gather x1, waiting for transfers between devices, gather_and_add(): parts = lax.all_gather(x, axis)  852 us
    psum x1, waiting for transfers between devices, shards(): gram_second = lax.psum(local_second, ('gx', 'gy', 'gz'))  270 us
    psum x1, waiting for transfers between devices, shards(): gram_third = lax.psum(local_third, ('gx', 'gy', 'gz'))  267 us
    all_to_all x1, blocking collectives, shards(): lax.all_to_all(grid_block, 'gx', split_axis=2, concat_axis=1, tiled=True)  39.6 us
  transfers between devices with their start and end apart: 3, of which 3 were waited for; matrix products, arithmetic and copies ran while one was open for 0% of the time, Pallas kernels for 0%

profile of v2, /device:TPU:24, one launch (start us, length us, event | category | flops | bytes accessed | tf_op | source)
XLA Modules:
  0.0 1587.3 jit_solution(10987002310511980648)
XLA Ops:
  6.6 1.6 copy.35
  10.6 20.2 %all_to_all.69 = f32[4,1,128,512]{2,0,1,3:T(4,128)S(1)} all-to-all(f32[4,1,128,512]{2,0,1,3:T(4,128)S(1)} %copy.38), channel_id=1, replica_groups=mesh['gx'=16,'gy'=4,'gz'=8] {'gz'}, dimensions={3} | all-to-all | bytes 2097152 | tf_op jit(solution)/shard_map/all_to_all | solution.py:44
  30.9 1.8 copy.40
  32.7 1.3 reshape.63
  34.0 39.6 %all_to_all.70 = f32[16,1,16384]{2,1,0:T(1,128)S(1)} all-to-all(f32[16,1,16384]{2,1,0:T(1,128)S(1)} %reshape.63), channel_id=1, replica_groups=mesh['gx'=16,'gy'=4,'gz'=8] {'gx'}, dimensions={0} | all-to-all | bytes 2097152 | tf_op jit(solution)/shard_map/all_to_all | solution.py:45
  74.1 3.1 reduce.4
  78.1 2.6 copy.42
  80.7 2.2 copy.43
  82.9 2.4 convolution_bitcast_fusion.6
  85.4 852.2 %all-gather.3.cloned.1.call-done = f32[65536,128]{1,0:T(8,128)} async-done(((f32[128,128]{1,0:T(8,128)}), f32[65536,128]{1,0:T(8,128)}) %all-gather.3.cloned.1.call-update) | async-done | bytes 33554448 | tf_op jit(solution)/shard_map/all_gather | solution.py:11
  937.6 13.1 reduce_sum.9
  951.2 2.9 cholesky.104
  955.6 2.4 custom-call.12
  958.7 2.9 cholesky.115
  963.1 2.4 custom-call.13
  965.8 2.9 convolution_bitcast_fusion.3
  969.4 20.7 %all_to_all.71 = f32[64,1,1024]{2,1,0:T(1,128)S(1)} all-to-all(f32[64,1,1024]{2,1,0:T(1,128)S(1)} %reshape.65), channel_id=1, replica_groups=mesh['gx'=16,'gy'=4,'gz'=8] {'gx','gy'}, dimensions={0} | all-to-all | bytes 524288 | tf_op jit(solution)/shard_map/all_to_all | solution.py:52
  991.5 2.1 convolution_bitcast_fusion.1
  993.7 270.1 %all-reduce.3.cloned.1.call-done = f32[512,512]{1,0:T(8,128)} async-done(((f32[512,512]{1,0:T(8,128)}), f32[512,512]{1,0:T(8,128)}) %all-reduce.3.cloned.1.call-update) | async-done | bytes 1048592 | tf_op jit(solution)/shard_map/psum | solution.py:59
  1263.7 2.4 fusion.41
  1266.4 2.9 cholesky.126
  1270.8 2.4 custom-call.14
  1274.9 2.9 cholesky.137
  1279.3 2.4 custom-call.15
  1282.5 9.2 all_to_all.72
  1292.6 2.1 convolution_bitcast_fusion
  1294.7 267.3 %all-reduce.5.cloned.1.call-done = f32[512,512]{1,0:T(8,128)} async-done(((f32[512,512]{1,0:T(8,128)}), f32[512,512]{1,0:T(8,128)}) %all-reduce.5.cloned.1.call-update) | async-done | bytes 1048592 | tf_op jit(solution)/shard_map/psum | solution.py:64
  1562.0 2.4 fusion.45
  1564.6 2.9 cholesky.148
  1568.9 2.4 custom-call.16
  1573.0 2.9 cholesky.159
  1577.3 2.4 custom-call.17
  (85 shorter events, 22.3 us)
Async XLA Ops:
  6.5 1257.2 %copy-start = (f32[512,32]{0,1:T(8,128)S(1)}, f32[512,32]{0,1:T(8,128)}, u32[]{:S(2)}) copy-start(f32[512,32]{0,1:T(8,128)} %param.13) | copy-start | bytes 196612
  6.5 1.6 copy-start.5
  6.5 931.1 %all-gather.3.cloned.1.call-start = ((), (), s32[]{:S(2)}) async-start(), calls=%async_computation.6 | async-start | bytes 33619968 | tf_op jit(solution)/shard_map/all_gather | solution.py:11
  85.3 1178.4 %all-reduce.3.cloned.1.call-start = ((), (), s32[]{:S(2)}) async-start(), calls=%async_computation.4 | async-start | bytes 2097152 | tf_op jit(solution)/shard_map/psum | solution.py:59
  937.6 13.1 copy-start.4
  993.6 568.4 %all-reduce.5.cloned.1.call-start = ((), (), s32[]{:S(2)}) async-start(), calls=%async_computation.5 | async-start | bytes 2097152 | tf_op jit(solution)/shard_map/psum | solution.py:64
  1263.7 9.8 copy-start.1
  1273.5 288.5 %copy-start.3 = (f32[512,32]{0,1:T(8,128)S(1)}, f32[512,32]{0,1:T(8,128)}, u32[]{:S(2)}) copy-start(f32[512,32]{0,1:T(8,128)} %param.14) | copy-start | bytes 196612
  1562.0 9.6 copy-start.2
Sparse Core Ops, SparseCore 0:
  85.5 852.1 all-gather.2
  993.7 269.9 all-reduce.2
  1294.8 267.1 all-reduce.4
